TPU v7x, 32 devices: a whole 2x2x4 slice. The times are simulated.
32 devices in a mesh: party: 2 (over x), dp: 16 (over z, y, core).
Axes of the slice: x: 2, y: 2, z: 4, core: 2. Of those that a mesh axis runs over, the one named last changes fastest.
Arguments:
- x_share: float32 [2, 8192, 1024], P('party', 'dp'), may hold values from -6 to 6
- w_share: float32 [2, 1024, 2048], P('party', 'dp'), may hold values from -0.1875 to 0.1875
- g_share: float32 [2, 8192, 2048], P('party', 'dp'), may hold values from -0.0625 to 0.0625
- fwd_a: float32 [2, 8192, 1024], P('party', 'dp'), may hold values from -4 to 4
- fwd_b: float32 [2, 1024, 2048], P('party', 'dp'), may hold values from -0.125 to 0.125
- fwd_c: float32 [2, 8192, 2048], P('party', 'dp'), may hold values from -2100 to 2100, as said below
- bwd_a: float32 [2, 8192, 1024], P('party', 'dp'), may hold values from -4 to 4
- bwd_b: float32 [2, 8192, 2048], P('party', 'dp'), may hold values from -0.044194174 to 0.044194174
- bwd_c: float32 [2, 1024, 2048], P('party', 'dp'), may hold values from -2100 to 2100, as said below
Outputs:
- y_share: float32 [2, 8192, 2048], P('party', 'dp')
- dw_share: float32 [2, 1024, 2048], P('party', 'dp')
Inputs may be any that keep to these rules, and one draw needn't show every extreme that they name: fwd_c[0] + fwd_c[1] equals (fwd_a[0] + fwd_a[1]) (fwd_b[0] + fwd_b[1]) up to float32 rounding. bwd_c[0] + bwd_c[1] equals (bwd_a[0] + bwd_a[1])^T (bwd_b[0] + bwd_b[1]) up to float32 rounding.
All inputs are finite; a program needn't handle non-finite values.
Results may differ from a plain program's by a relative error of at most 0.0001.
Values sent between devices are 32-bit elements; how exact they have to be, the bound alone decides.
A program may use at most 128 MiB of HBM per device.

v0:
```python
import jax
import jax.numpy as jnp
from jax import lax
from jax.sharding import PartitionSpec as P


def matmul(left, right):
    return jnp.dot(left, right, preferred_element_type=jnp.float32, precision=lax.Precision.HIGHEST)


def tmatmul(left, right):
    return lax.dot_general(
        left,
        right,
        (((0,), (0,)), ((), ())),
        precision=lax.Precision.HIGHEST,
        preferred_element_type=jnp.float32,
    )


def body(x_share, w_share, g_share, fwd_a, fwd_b, fwd_c, bwd_a, bwd_b, bwd_c):
    first = (lax.axis_index("party") == 0).astype(jnp.float32)
    inputs = x_share[0]
    left_fwd = fwd_a[0]
    eps_fwd = lax.psum(inputs - left_fwd, "party")
    delta_rows = lax.psum(w_share[0] - fwd_b[0], "party")
    corrected_fwd, delta_fwd = (
        lax.all_gather(fwd_b[0] + first * delta_rows, "dp", axis=0, tiled=True),
        lax.all_gather(delta_rows, "dp", axis=0, tiled=True),
    )
    outputs = fwd_c[0] + matmul(eps_fwd, corrected_fwd) + matmul(left_fwd, delta_fwd)
    left_bwd = bwd_a[0]
    eps_bwd, delta_bwd = lax.psum((inputs - left_bwd, g_share[0] - bwd_b[0]), "party")
    corrected = bwd_b[0] + first * delta_bwd
    partial_value = tmatmul(eps_bwd, corrected) + tmatmul(left_bwd, delta_bwd)
    summed = lax.psum_scatter(partial_value, "dp", scatter_dimension=0, tiled=True)
    return (outputs[None], (bwd_c[0] + summed)[None])


def solution(mesh):
    in_specs = (
        P("party", "dp", None),
        P("party", "dp", None),
        P("party", "dp", None),
        P("party", "dp", None),
        P("party", "dp", None),
        P("party", "dp", None),
        P("party", "dp", None),
        P("party", "dp", None),
        P("party", "dp", None),
    )
    out_specs = (P("party", "dp", None), P("party", "dp", None))
    return jax.shard_map(body, mesh=mesh, in_specs=in_specs, out_specs=out_specs, check_vma=False)
```

profile of v0, /device:TPU:0, one launch (start us, length us, event | category | flops | bytes accessed | tf_op | source)
XLA Modules:
  0.0 543.7 jit_solution(15295625302415227886)
XLA Ops:
  7.2 0.0 copy-start.7
  7.2 0.0 copy-start.5
  7.2 0.0 copy-start.1
  7.2 0.0 all-reduce.3.cloned.1.call-start
  7.2 0.0 copy-start.2
  7.3 0.0 copy-start.4
  7.3 6.7 %bitcast_subtract_fusion = f32[512,2048]{1,0:T(8,128)} fusion(f32[1,512,2048]{2,1,0:T(8,128)} %param.11, f32[1,512,2048]{2,1,0:T(8,128)} %param.16), kind=kLoop, calls=%fused_computation.1 | loop fusion | flops 1048576 | bytes 12582912 | tf_op jit(solution)/shard_map/sub | solution.py:33
  14.0 0.0 copy-done.7
  14.0 0.0 copy-done.5
  14.0 0.8 bitcast_subtract_fusion.3
  14.8 0.0 copy-done.1
  14.8 0.0 copy-done.2
  14.8 0.0 copy-done.4
  14.8 2.7 bitcast_subtract_fusion.1
  17.6 0.0 all-reduce.3.cloned.1.call-update
  17.6 0.0 reduce-scatter.2.cloned.1.call-start
  17.6 212.2 %all-reduce.3.cloned.1.call-done = (f32[512,1024]{1,0:T(8,128)}, f32[64,2048]{1,0:T(8,128)}, f32[512,1024]{1,0:T(8,128)}, f32[512,2048]{1,0:T(8,128)}) async-done(((f32[512,1024]{1,0:T(8,128)}, f32[64,2048]{1,0:T(8,128)}, f32[512,1024]{1,0:T(8,128)}, f32[512,2048]{1,0:T(8,128)}), (f32[512,1024]{1,0:T(8,128)}, f32[64,2048]{1,0:T(8,128)}, f32[512,1024]{1,0:T(8,128)}, ...) | async-done | bytes 8912912 | tf_op jit(solution)/shard_map/psum | solution.py:25
  229.8 0.0 copy-start
  229.9 17.6 %fusion = f32[1024,2048]{1,0:T(8,128)S(1)} fusion(f32[512,1024]{1,0:T(8,128)} %get-tuple-element.4, f32[1,512,2048]{2,1,0:T(8,128)} %param.16, f32[512,2048]{1,0:T(8,128)} %get-tuple-element.5, f32[]{:T(128)S(6)} %convert_element_type.3), kind=kOutput, calls=%fused_computation.3 | convolution fusion | flops 12886999040 | bytes 18874372 | tf_op jit(solution)/shard_map/dot_general | solution.py:12
  247.5 0.0 copy-done
  247.5 16.4 %bitcast_add_fusion = f32[1024,2048]{1,0:T(8,128)} fusion(f32[1024,2048]{1,0:T(8,128)S(1)} %fusion, f32[512,2048]{1,0:T(8,128)S(1)} %copy-done, f32[1,512,1024]{2,1,0:T(8,128)S(1)} %copy-done.1), kind=kOutput, calls=%fused_computation | convolution fusion | flops 12886999040 | bytes 23068672 | tf_op jit(solution)/shard_map/dot_general | solution.py:12
  263.9 0.0 copy-start.6
  263.9 0.0 copy-start.8
  263.9 0.0 reduce-scatter.2.cloned.1.call-update
  263.9 0.0 all-gather.3.cloned.1.call-start
  264.0 1.0 copy-done.6
  264.9 0.8 bitcast_add_fusion.6
  265.8 0.0 all-gather.3.cloned.1.call-update
  265.8 0.0 all-gather.5.cloned.1.call-start
  265.9 0.5 all-gather.5.cloned.1.call-update
  266.4 101.8 %reduce-scatter.2.cloned.1.call-done = f32[64,2048]{1,0:T(8,128)} async-done(((f32[1024,2048]{1,0:T(8,128)}), f32[64,2048]{1,0:T(8,128)}) %reduce-scatter.2.cloned.1.call-update) | async-done | bytes 524304 | tf_op jit(solution)/shard_map/reduce_scatter | solution.py:36
  368.2 0.0 copy-done.8
  368.2 1.9 fusion.6
  370.1 74.8 %all-gather.3.cloned.1.call-done = f32[1024,2048]{1,0:T(8,128)} async-done(((f32[64,2048]{1,0:T(8,128)}), f32[1024,2048]{1,0:T(8,128)}) %all-gather.3.cloned.1.call-update) | async-done | bytes 8388624 | tf_op jit(solution)/shard_map/all_gather | solution.py:28
  444.9 0.0 copy-start.3
  444.9 18.1 %fusion.7 = f32[512,2048]{1,0:T(8,128)} fusion(f32[512,1024]{1,0:T(8,128)} %get-tuple-element.2, f32[1024,2048]{1,0:T(8,128)} %all-gather.3.cloned.1.call-done), kind=kOutput, calls=%fused_computation.17 | convolution fusion | flops 12884901888 | bytes 14680064 | tf_op jit(solution)/shard_map/dot_general | solution.py:8
  463.1 56.8 %all-gather.5.cloned.1.call-done = f32[1024,2048]{1,0:T(8,128)} async-done(((f32[64,2048]{1,0:T(8,128)}), f32[1024,2048]{1,0:T(8,128)}) %all-gather.5.cloned.1.call-update) | async-done | bytes 8388624 | tf_op jit(solution)/shard_map/all_gather | solution.py:29
  519.9 0.0 copy-done.3
  519.9 17.3 %fusion.1 = f32[1,512,2048]{2,1,0:T(8,128)} fusion(f32[512,2048]{1,0:T(8,128)} %fusion.7, f32[1,512,2048]{2,1,0:T(8,128)} %param.14, f32[1024,2048]{1,0:T(8,128)} %all-gather.5.cloned.1.call-done, f32[1,512,1024]{2,1,0:T(8,128)S(1)} %copy-done.3), kind=kOutput, calls=%fused_computation.5 | convolution fusion | flops 12886999040 | bytes 23068672 | tf_op jit(solution)/shard_map/dot_general | solution.py:8
Async XLA Ops:
  7.2 6.8 %copy-start.7 = (f32[1,64,2048]{2,1,0:T(8,128)S(1)}, f32[1,64,2048]{2,1,0:T(8,128)}, u32[]{:S(2)}) copy-start(f32[1,64,2048]{2,1,0:T(8,128)} %param.10) | copy-start | bytes 1572868
  7.2 6.8 %copy-start.5 = (f32[1,64,2048]{2,1,0:T(8,128)S(1)}, f32[1,64,2048]{2,1,0:T(8,128)}, u32[]{:S(2)}) copy-start(f32[1,64,2048]{2,1,0:T(8,128)} %param.13) | copy-start | bytes 1572868
  7.2 7.6 %copy-start.1 = (f32[1,512,1024]{2,1,0:T(8,128)S(1)}, f32[1,512,1024]{2,1,0:T(8,128)}, u32[]{:S(2)}) copy-start(f32[1,512,1024]{2,1,0:T(8,128)} %param.15) | copy-start | bytes 6291460
  7.2 222.7 %all-reduce.3.cloned.1.call-start = ((), (), s32[]{:S(2)}) async-start(), calls=%async_computation.4 | async-start | bytes 17825792 | tf_op jit(solution)/shard_map/psum | solution.py:25
  7.2 7.6 %copy-start.2 = (f32[1,512,1024]{2,1,0:T(8,128)S(1)}, f32[1,512,1024]{2,1,0:T(8,128)}, u32[]{:S(2)}) copy-start(f32[1,512,1024]{2,1,0:T(8,128)} %param.12) | copy-start | bytes 6291460
  7.3 7.6 %copy-start.4 = (f32[1,512,1024]{2,1,0:T(8,128)S(1)}, f32[1,512,1024]{2,1,0:T(8,128)}, u32[]{:S(2)}) copy-start(f32[1,512,1024]{2,1,0:T(8,128)} %param.9) | copy-start | bytes 6291460
  17.6 350.6 %reduce-scatter.2.cloned.1.call-start = ((), (), s32[]{:S(2)}) async-start(), calls=%async_computation.3 | async-start | bytes 8912896 | tf_op jit(solution)/shard_map/reduce_scatter | solution.py:36
  229.8 17.7 %copy-start = (f32[512,2048]{1,0:T(8,128)S(1)}, f32[512,2048]{1,0:T(8,128)}, u32[]{:S(2)}) copy-start(f32[512,2048]{1,0:T(8,128)} %get-tuple-element.5) | copy-start | bytes 12582916
  263.9 1.0 copy-start.6
  263.9 104.3 %copy-start.8 = (f32[1,64,2048]{2,1,0:T(8,128)S(1)}, f32[1,64,2048]{2,1,0:T(8,128)}, u32[]{:S(2)}) copy-start(f32[1,64,2048]{2,1,0:T(8,128)} %param.17) | copy-start | bytes 1572868
  263.9 181.0 %all-gather.3.cloned.1.call-start = ((), (), s32[]{:S(2)}) async-start(), calls=%async_computation.1 | async-start | bytes 8912896 | tf_op jit(solution)/shard_map/all_gather | solution.py:28
  265.8 254.0 %all-gather.5.cloned.1.call-start = ((), (), s32[]{:S(2)}) async-start(), calls=%async_computation.2 | async-start | bytes 8912896 | tf_op jit(solution)/shard_map/all_gather | solution.py:29
  444.9 74.9 %copy-start.3 = (f32[1,512,1024]{2,1,0:T(8,128)S(1)}, f32[1,512,1024]{2,1,0:T(8,128)}, u32[]{:S(2)}) copy-start(f32[1,512,1024]{2,1,0:T(8,128)} %param.12) | copy-start | bytes 6291460
Sparse Core Ops, SparseCore 0:
  17.7 212.1 all-reduce.2
  264.1 104.1 reduce-scatter.1
  371.0 73.9 all-gather.2
  447.0 72.8 all-gather.4
where the time goes:
time: 544 us
  waiting for transfers between devices  446 us (82%)
  matrix products  69.5 us (13%)
  between operations  13.8 us (3%)
  other arithmetic  13 us (2%)
    psum x1, waiting for transfers between devices, body(): eps_fwd = lax.psum(inputs - left_fwd, 'party')  212 us
    reduce_scatter x1, waiting for transfers between devices, body(): lax.psum_scatter(partial_value, 'dp', scatter_dimension=0, tiled=True)  102 us
    all_gather x1, waiting for transfers between devices, body(): lax.all_gather(fwd_b[0] + first * delta_rows, 'dp', axis=0, tiled=True)  74.8 us
    all_gather x1, waiting for transfers between devices, body(): lax.all_gather(delta_rows, 'dp', axis=0, tiled=True)  56.8 us
    dot_general x2, matrix products, matmul(): jnp.dot(left, right, preferred_element_type=jnp.float32, precision=lax.Pr...  35.4 us
    dot_general x2, matrix products, tmatmul(): lax.dot_general(left, right, (((0,), (0,)), ((), ())), precision=lax.Prec...  34 us
  transfers between devices with their start and end apart: 4, of which 4 were waited for; matrix products, arithmetic and copies ran while one was open for 4% of the time, Pallas kernels for 0%

commit v1 on v0

--- a/solution.py
+++ b/solution.py
@@ -22,7 +22,9 @@
     first = (lax.axis_index("party") == 0).astype(jnp.float32)
     inputs = x_share[0]
     left_fwd = fwd_a[0]
-    eps_fwd = lax.psum(inputs - left_fwd, "party")
+    own = inputs - left_fwd
+    blocks = lax.all_gather(own, "party")
+    eps_fwd = jnp.sum(blocks, axis=0)
     delta_rows = lax.psum(w_share[0] - fwd_b[0], "party")
     corrected_fwd, delta_fwd = (
         lax.all_gather(fwd_b[0] + first * delta_rows, "dp", axis=0, tiled=True),

time: 544 us -> 527 us (0.969)
  waiting for transfers between devices: 446 us -> 423 us
    psum x1, waiting for transfers between devices: 212 us -> 164 us  [body(): delta_rows = lax.psum(w_share[0] - fwd_b[0], 'party')]
    all_gather x0 -> x1, waiting for transfers between devices: none -> 21.3 us  [body(): blocks = lax.all_gather(own, 'party')]
  transfers between devices with their start and end apart: 4 -> 5, of which waited for: 4 -> 5; matrix products, arithmetic and copies ran while one was open for 4% -> 12% of each run, Pallas kernels for 0% -> 0%
where the time goes in v1:
time: 527 us; the launch traced here: 526 us
  waiting for transfers between devices  423 us (80%)
  matrix products  70 us (13%)
  other arithmetic  18.2 us (3%)
  between operations  13.8 us (3%)
    psum x1, waiting for transfers between devices, body(): delta_rows = lax.psum(w_share[0] - fwd_b[0], 'party')  164 us
    reduce_scatter x1, waiting for transfers between devices, body(): lax.psum_scatter(partial_value, 'dp', scatter_dimension=0, tiled=True)  105 us
    all_gather x1, waiting for transfers between devices, body(): lax.all_gather(fwd_b[0] + first * delta_rows, 'dp', axis=0, tiled=True)  74.7 us
    all_gather x1, waiting for transfers between devices, body(): lax.all_gather(delta_rows, 'dp', axis=0, tiled=True)  57.6 us
    dot_general x2, matrix products, matmul(): jnp.dot(left, right, preferred_element_type=jnp.float32, precision=lax.Pr...  35.6 us
    dot_general x2, matrix products, tmatmul(): lax.dot_general(left, right, (((0,), (0,)), ((), ())), precision=lax.Prec...  34.4 us
    all_gather x1, waiting for transfers between devices, body(): blocks = lax.all_gather(own, 'party')  21.3 us
  transfers between devices with their start and end apart: 5, of which 5 were waited for; matrix products, arithmetic and copies ran while one was open for 12% of the time, Pallas kernels for 0%

profile of v1, /device:TPU:0, one launch (start us, length us, event | category | flops | bytes accessed | tf_op | source)
XLA Modules:
  0.0 526.3 jit_solution(15168326984914676289)
XLA Ops:
  7.2 0.0 copy-start.1
  7.2 0.0 all-reduce.3.cloned.1.call-start
  7.2 0.0 copy-start.2
  7.2 6.7 %bitcast_subtract_fusion = f32[512,2048]{1,0:T(8,128)} fusion(f32[1,512,2048]{2,1,0:T(8,128)} %param.11, f32[1,512,2048]{2,1,0:T(8,128)} %param.16), kind=kLoop, calls=%fused_computation.1 | loop fusion | flops 1048576 | bytes 12582912 | tf_op jit(solution)/shard_map/sub | solution.py:35
  13.9 0.0 copy-done.1
  13.9 0.0 copy-done.2
  13.9 0.0 copy-start.4
  13.9 0.0 copy-start.6
  14.0 1.7 bitcast_subtract_fusion.1
  15.7 0.0 copy-done.4
  15.7 0.0 copy-done.6
  15.7 0.9 bitcast_subtract_fusion.2
  16.6 0.0 all-reduce.3.cloned.1.call-update
  16.6 0.0 all-gather.4.cloned.1.call-start
  16.6 3.3 sub.13
  20.0 0.0 all-gather.4.cloned.1.call-update
  20.0 0.0 reduce-scatter.2.cloned.1.call-start
  20.1 164.0 %all-reduce.3.cloned.1.call-done = (f32[64,2048]{1,0:T(8,128)}, f32[512,1024]{1,0:T(8,128)}, f32[512,2048]{1,0:T(8,128)}) async-done(((f32[64,2048]{1,0:T(8,128)}, f32[512,1024]{1,0:T(8,128)}, f32[512,2048]{1,0:T(8,128)}), (f32[64,2048]{1,0:T(8,128)}, f32[512,1024]{1,0:T(8,128)}, f32[512,2048]{1,0:T(8,128)})) %all-reduce.3.cloned.1.call-update) | async-done | bytes 6815760 | tf_op jit(solution)/shard_map/psum | solution.py:28
  184.1 0.0 copy-start
  184.1 0.0 copy-start.3
  184.1 17.6 %fusion = f32[1024,2048]{1,0:T(8,128)S(1)} fusion(f32[512,1024]{1,0:T(8,128)} %get-tuple-element.3, f32[1,512,2048]{2,1,0:T(8,128)} %param.16, f32[512,2048]{1,0:T(8,128)} %get-tuple-element.4, f32[]{:T(128)S(6)} %convert_element_type.3), kind=kOutput, calls=%fused_computation.3 | convolution fusion | flops 12886999040 | bytes 18874372 | tf_op jit(solution)/shard_map/dot_general | solution.py:12
  201.7 0.0 copy-done
  201.7 0.0 copy-done.3
  201.7 16.8 %bitcast_add_fusion = f32[1024,2048]{1,0:T(8,128)} fusion(f32[1024,2048]{1,0:T(8,128)S(1)} %fusion, f32[512,2048]{1,0:T(8,128)S(1)} %copy-done, f32[1,512,1024]{2,1,0:T(8,128)S(1)} %copy-done.3), kind=kOutput, calls=%fused_computation | convolution fusion | flops 12886999040 | bytes 23068672 | tf_op jit(solution)/shard_map/dot_general | solution.py:12
  218.5 0.0 copy-start.5
  218.5 0.0 reduce-scatter.2.cloned.1.call-update
  218.6 0.0 all-gather.6.cloned.1.call-start
  218.6 1.0 copy-done.5
  219.6 0.8 bitcast_add_fusion.6
  220.4 0.0 copy-start.7
  220.4 0.0 all-gather.6.cloned.1.call-update
  220.4 0.0 all-gather.8.cloned.1.call-start
  220.5 0.5 all-gather.8.cloned.1.call-update
  221.0 21.3 %all-gather.4.cloned.1.call-done = f32[2,512,1024]{2,1,0:T(8,128)} async-done(((f32[1,512,1024]{2,1,0:T(8,128)}), f32[2,512,1024]{2,1,0:T(8,128)}) %all-gather.4.cloned.1.call-update) | async-done | bytes 4194320 | tf_op jit(solution)/shard_map/all_gather | solution.py:26
  242.4 2.8 reduce_sum.9
  245.2 104.7 %reduce-scatter.2.cloned.1.call-done = f32[64,2048]{1,0:T(8,128)} async-done(((f32[1024,2048]{1,0:T(8,128)}), f32[64,2048]{1,0:T(8,128)}) %reduce-scatter.2.cloned.1.call-update) | async-done | bytes 524304 | tf_op jit(solution)/shard_map/reduce_scatter | solution.py:38
  349.9 0.0 copy-done.7
  349.9 1.9 fusion.6
  351.8 74.7 %all-gather.6.cloned.1.call-done = f32[1024,2048]{1,0:T(8,128)} async-done(((f32[64,2048]{1,0:T(8,128)}), f32[1024,2048]{1,0:T(8,128)}) %all-gather.6.cloned.1.call-update) | async-done | bytes 8388624 | tf_op jit(solution)/shard_map/all_gather | solution.py:30
  426.5 17.3 %fusion.7 = f32[512,2048]{1,0:T(8,128)} fusion(f32[512,1024]{1,0:T(8,128)S(1)} %reduce_sum.9, f32[1024,2048]{1,0:T(8,128)} %all-gather.6.cloned.1.call-done), kind=kOutput, calls=%fused_computation.16 | convolution fusion | flops 12884901888 | bytes 14680064 | tf_op jit(solution)/shard_map/dot_general | solution.py:8
  443.8 57.6 %all-gather.8.cloned.1.call-done = f32[1024,2048]{1,0:T(8,128)} async-done(((f32[64,2048]{1,0:T(8,128)}), f32[1024,2048]{1,0:T(8,128)}) %all-gather.8.cloned.1.call-update) | async-done | bytes 8388624 | tf_op jit(solution)/shard_map/all_gather | solution.py:31
  501.4 18.3 %fusion.1 = f32[1,512,2048]{2,1,0:T(8,128)} fusion(f32[512,2048]{1,0:T(8,128)} %fusion.7, f32[1,512,2048]{2,1,0:T(8,128)} %param.14, f32[1024,2048]{1,0:T(8,128)} %all-gather.8.cloned.1.call-done, f32[1,512,1024]{2,1,0:T(8,128)} %param.12), kind=kOutput, calls=%fused_computation.5 | convolution fusion | flops 12886999040 | bytes 23068672 | tf_op jit(solution)/shard_map/dot_general | solution.py:8
Async XLA Ops:
  7.2 6.8 %copy-start.1 = (f32[1,512,1024]{2,1,0:T(8,128)S(1)}, f32[1,512,1024]{2,1,0:T(8,128)}, u32[]{:S(2)}) copy-start(f32[1,512,1024]{2,1,0:T(8,128)} %param.9) | copy-start | bytes 6291460
  7.2 176.9 %all-reduce.3.cloned.1.call-start = ((), (), s32[]{:S(2)}) async-start(), calls=%async_computation.5 | async-start | bytes 13631488 | tf_op jit(solution)/shard_map/psum | solution.py:28
  7.2 6.7 %copy-start.2 = (f32[1,512,1024]{2,1,0:T(8,128)S(1)}, f32[1,512,1024]{2,1,0:T(8,128)}, u32[]{:S(2)}) copy-start(f32[1,512,1024]{2,1,0:T(8,128)} %param.15) | copy-start | bytes 6291460
  13.9 1.8 copy-start.4
  13.9 1.8 copy-start.6
  16.6 225.8 %all-gather.4.cloned.1.call-start = ((), (), s32[]{:S(2)}) async-start(), calls=%async_computation.1 | async-start | bytes 6291456 | tf_op jit(solution)/shard_map/all_gather | solution.py:26
  20.0 329.9 %reduce-scatter.2.cloned.1.call-start = ((), (), s32[]{:S(2)}) async-start(), calls=%async_computation.4 | async-start | bytes 8912896 | tf_op jit(solution)/shard_map/reduce_scatter | solution.py:38
  184.1 17.7 %copy-start = (f32[512,2048]{1,0:T(8,128)S(1)}, f32[512,2048]{1,0:T(8,128)}, u32[]{:S(2)}) copy-start(f32[512,2048]{1,0:T(8,128)} %get-tuple-element.4) | copy-start | bytes 12582916
  184.1 17.7 %copy-start.3 = (f32[1,512,1024]{2,1,0:T(8,128)S(1)}, f32[1,512,1024]{2,1,0:T(8,128)}, u32[]{:S(2)}) copy-start(f32[1,512,1024]{2,1,0:T(8,128)} %param.15) | copy-start | bytes 6291460
  218.5 1.0 copy-start.5
  218.6 207.9 %all-gather.6.cloned.1.call-start = ((), (), s32[]{:S(2)}) async-start(), calls=%async_computation.2 | async-start | bytes 8912896 | tf_op jit(solution)/shard_map/all_gather | solution.py:30
  220.4 129.5 %copy-start.7 = (f32[1,64,2048]{2,1,0:T(8,128)S(1)}, f32[1,64,2048]{2,1,0:T(8,128)}, u32[]{:S(2)}) copy-start(f32[1,64,2048]{2,1,0:T(8,128)} %param.17) | copy-start | bytes 1572868
  220.4 281.0 %all-gather.8.cloned.1.call-start = ((), (), s32[]{:S(2)}) async-start(), calls=%async_computation.3 | async-start | bytes 8912896 | tf_op jit(solution)/shard_map/all_gather | solution.py:31
Sparse Core Ops, SparseCore 0:
  16.7 167.3 all-reduce.2
  185.6 56.7 all-gather.3
  246.4 103.4 reduce-scatter.1
  352.5 73.9 all-gather.5
  428.5 72.8 all-gather.7
